TPU v7x, 32 devices: a whole 2x2x4 slice. The times are simulated.
32 devices in a mesh: row: 4 (over y, core), col: 8 (over z, x).
Axes of the slice: x: 2, y: 2, z: 4, core: 2. Of those that a mesh axis runs over, the one named last changes fastest.
Arguments:
- adjoint_field: float32 [5, 6, 192, 3072], P(None, None, 'row', 'col'), may hold values from -6 to 6
- advect_x: float32 [6, 192, 3072], P(None, 'row', 'col'), may hold values from -0.8 to 0.8
- advect_y: float32 [6, 192, 3072], P(None, 'row', 'col'), may hold values from -0.8 to 0.8
- diffusion: float32 [5, 6, 192, 3072], P(None, None, 'row', 'col'), may hold values from 0.02 to 0.2
- zone_cells: int32 [4], replicated, may hold values from 2 to 6
- feedback_dest: int32 [8, 64, 1], P('col', 'row'), may hold values from 0 to 7; in each aligned block of 16 rows (0 to 15, 16 to 31, ..., all dimensions but the last counted through in order) at most 2 rows name the same one
- feedback_slot: int32 [8, 64, 1], P('col', 'row'), may hold values from 0 to 79
Outputs:
- nest_adjoint: float32 [5, 6, 192, 3072], P(None, None, 'row', 'col')
- parent_adjoint: float32 [5, 6, 320, 1024], P(None, None, 'row', 'col')
Inputs may be any that keep to these rules, and one draw needn't show every extreme that they name: `feedback_dest`: the 16 feedback rows of one device name one destination at most 2 times, a bound that some block reaches.
All inputs are finite; a program needn't handle non-finite values.
Results may differ from a plain program's by a relative error of at most 0.00012.
Values sent between devices are 32-bit elements; how exact they have to be, the bound alone decides.
A program may use at most 192 MiB of HBM per device.

v0:
```python
import jax
import jax.numpy as jnp
from jax import lax
from jax.sharding import PartitionSpec as P

ITERS = 3
PROWS = 80
CAP = 2


def with_halo(cells, sides, width):
    for axis, dim in sides:
        count = lax.axis_size(axis)
        ends = count - 1
        head = lax.slice_in_dim(cells, 0, width, axis=dim)
        tail = lax.slice_in_dim(cells, cells.shape[dim] - width, cells.shape[dim], axis=dim)
        cells = jnp.concatenate(
            [
                lax.ppermute(tail, axis, [(i, (i + 1) % count) for i in range(ends)]),
                cells,
                lax.ppermute(head, axis, [((i + 1) % count, i) for i in range(ends)]),
            ],
            axis=dim,
        )
    return cells


def advance(widened, coef_x, coef_y, coef_d):
    flux_x = coef_x * widened
    flux_y = coef_y * widened
    spread = coef_d * widened
    center = widened[..., 1:-1, 1:-1]
    result = center + 0.5 * (flux_x[..., 2:, 1:-1] - flux_x[..., :-2, 1:-1])
    result = result + 0.5 * (flux_y[..., 1:-1, 2:] - flux_y[..., 1:-1, :-2])
    result = result + spread[..., 2:, 1:-1] + spread[..., :-2, 1:-1]
    result = result + spread[..., 1:-1, 2:] + spread[..., 1:-1, :-2]
    return result - 4.0 * spread[..., 1:-1, 1:-1]


def ramp_weight(offset, count, total, low_zone, high_zone):
    positions = offset + jnp.arange(count, dtype=jnp.int32)
    lower = jnp.maximum(low_zone - positions, 0).astype(jnp.float32) / (low_zone + 1).astype(
        jnp.float32
    )
    upper = jnp.maximum(high_zone - (total - 1 - positions), 0).astype(jnp.float32) / (
        high_zone + 1
    ).astype(jnp.float32)
    return jnp.maximum(lower, upper)


def shards(adjoint_field, advect_x, advect_y, diffusion, zone_cells, feedback_dest, feedback_slot):
    fields, levels, tile_rows, tile_cols = adjoint_field.shape
    planes = fields * levels
    row_index = lax.axis_index("row")
    col_index = lax.axis_index("col")
    grid_rows = tile_rows * lax.axis_size("row")
    grid_cols = tile_cols * lax.axis_size("col")
    coef_stack = jnp.concatenate(
        [diffusion.reshape(planes, tile_rows, tile_cols), advect_x, advect_y], 0
    )
    coef_wide = with_halo(coef_stack, (("row", 1), ("col", 2)), 1)
    spread_wide = coef_wide[:planes].reshape(fields, levels, tile_rows + 2, tile_cols + 2)
    along_rows = coef_wide[planes : planes + levels]
    along_cols = coef_wide[planes + levels :]
    field_now = adjoint_field
    for sweep in range(ITERS):
        widened = with_halo(
            field_now.reshape(planes, tile_rows, tile_cols), (("row", 1), ("col", 2)), 1
        )
        widened = widened.reshape(fields, levels, tile_rows + 2, tile_cols + 2)
        field_now = advance(widened, along_rows, along_cols, spread_wide)
    weight_rows = ramp_weight(
        row_index * tile_rows, tile_rows, grid_rows, zone_cells[0], zone_cells[1]
    )
    weight_cols = ramp_weight(
        col_index * tile_cols, tile_cols, grid_cols, zone_cells[2], zone_cells[3]
    )
    relaxation = jnp.maximum(weight_rows[:, None], weight_cols[None, :])
    nest_adjoint = (1.0 - relaxation) * field_now
    weighting = (1.0 - relaxation) / 9.0 + relaxation
    coarse_rows = tile_rows // 3
    coarse_cols = tile_cols // 3
    coarse = (
        (weighting * field_now).reshape(planes, coarse_rows, 3, coarse_cols, 3).sum(axis=(2, 4))
    )
    owners = feedback_dest.reshape(coarse_rows)
    parent_rows = feedback_slot.reshape(coarse_rows)
    row_slots = jnp.arange(PROWS, dtype=jnp.int32)
    tile_count = lax.axis_size("col")
    outgoing = tile_count * CAP
    ordinal = jnp.arange(coarse_rows, dtype=jnp.int32)
    matches = owners[:, None] == owners[None, :]
    earlier = ordinal[None, :] < ordinal[:, None]
    order_rank = jnp.sum((matches & earlier).astype(jnp.int32), axis=1)
    target_slot = owners * CAP + order_rank
    selector = (jnp.arange(outgoing, dtype=jnp.int32)[:, None] == target_slot[None, :]).astype(
        jnp.float32
    )
    outbound = jnp.einsum("kg,agc->kac", selector, coarse, precision=lax.Precision.HIGHEST)
    outbound = outbound.reshape(tile_count, CAP, planes, coarse_cols)
    tags = jnp.dot(selector, (parent_rows + 1).astype(jnp.float32), precision=lax.Precision.HIGHEST)
    tags = tags.reshape(tile_count, CAP)
    arrived, arrived_tags = (
        lax.all_to_all(outbound, "col", split_axis=0, concat_axis=0, tiled=True),
        lax.all_to_all(tags, "col", split_axis=0, concat_axis=0, tiled=True),
    )
    picker = (
        arrived_tags.reshape(outgoing)[None, :] == (row_slots + 1).astype(jnp.float32)[:, None]
    ).astype(jnp.float32)
    parent = jnp.einsum(
        "pk,kac->apc",
        picker,
        arrived.reshape(outgoing, planes, coarse_cols),
        precision=lax.Precision.HIGHEST,
    )
    parent_adjoint = parent.reshape(fields, levels, PROWS, coarse_cols)
    return (nest_adjoint, parent_adjoint)


def solution(mesh):
    placed = (
        P(None, None, "row", "col"),
        P(None, "row", "col"),
        P(None, "row", "col"),
        P(None, None, "row", "col"),
        P(),
        P("col", "row", None),
        P("col", "row", None),
    )
    return jax.shard_map(
        shards,
        mesh=mesh,
        in_specs=placed,
        out_specs=(P(None, None, "row", "col"), P(None, None, "row", "col")),
        check_vma=False,
    )
```

profile of v0, /device:TPU:1, one launch (start us, length us, event | category | flops | bytes accessed | tf_op | source)
XLA Modules:
  0.0 250.9 jit_solution(11661358675818106469)
XLA Ops:
  3.9 4.5 %collective-permute-start = (f32[30,1,384]{2,1,0:T(1,128)S(1)}, f32[30,1,384]{2,1,0:T(1,128)S(1)}, u32[]{:S(2)}, u32[]{:S(2)}) collective-permute-start(f32[30,1,384]{2,1,0:T(1,128)S(1)} %get-tuple-element.29), channel_id=1, source_target_pairs={{0,8},{8,16},{16,24},{1,9},{9,17},{17,25},{2,10},{10,18},{18,26},{... | collective-permute-start | bytes 138248 | tf_op jit(solution)/shard_map/ppermute | solution.py:19
  11.7 3.6 %collective-permute-start.4 = (f32[42,1,384]{2,1,0:T(1,128)S(1)}, f32[42,1,384]{2,1,0:T(1,128)S(1)}, u32[]{:S(2)}, u32[]{:S(2)}) collective-permute-start(f32[42,1,384]{2,1,0:T(1,128)S(1)} %get-tuple-element.17), channel_id=1, source_target_pairs={{0,8},{8,16},{16,24},{1,9},{9,17},{17,25},{2,10},{10,18},{18,26},{... | collective-permute-start | bytes 193544 | tf_op jit(solution)/shard_map/ppermute | solution.py:19
  21.6 4.0 %collective-permute-start.2 = (f32[30,50,1]{1,2,0:T(1,128)S(1)}, f32[30,50,1]{1,2,0:T(1,128)S(1)}, u32[]{:S(2)}, u32[]{:S(2)}) collective-permute-start(f32[30,50,1]{1,2,0:T(1,128)S(1)} %copy.93), channel_id=1, source_target_pairs={{0,1},{1,2},{2,3},{3,4},{4,5},{5,6},{6,7},{8,9},{9,10},{10,11},{11... | collective-permute-start | bytes 18008 | tf_op jit(solution)/shard_map/ppermute | solution.py:19
  26.6 5.4 %all-to-all-start.1 = ((f32[8,1,2]{2,1,0:T(1,128)}), f32[8,1,2]{2,1,0:T(1,128)}, u32[]{:S(2)}, u32[]{:S(2)}) async-start(f32[8,1,2]{2,1,0:T(1,128)} %copy.113), calls=%async_computation.1 | async-start | bytes 8192 | tf_op jit(solution)/shard_map/all_to_all | solution.py:105
  41.6 4.0 %collective-permute-start.6 = (f32[42,50,1]{1,0,2:T(8,128)S(1)}, f32[42,50,1]{1,0,2:T(8,128)S(1)}, u32[]{:S(2)}, u32[]{:S(2)}) collective-permute-start(f32[42,50,1]{1,0,2:T(8,128)S(1)} %copy.97), channel_id=1, source_target_pairs={{0,1},{1,2},{2,3},{3,4},{4,5},{5,6},{6,7},{8,9},{9,10},{10,11},{11... | collective-permute-start | bytes 25208 | tf_op jit(solution)/shard_map/ppermute | solution.py:19
  45.6 5.1 %pad_maximum_fusion.6 = f32[30,50,386]{2,1,0:T(8,128)} fusion(f32[30,50,1]{2,1,0:T(8,128)S(1)} %copy-done.13, f32[30,1,384]{2,1,0:T(1,128)S(1)} %collective-permute-done.1, f32[30,48,384]{2,1,0:T(8,128)} %bitcast.61, f32[30,1,384]{2,1,0:T(1,128)S(1)} %collective-permute-done, f32[30,50,1]{2,1,0:T(8,128)} %copy.95), kind=kLoop, calls=%fused_computation.6 | loop fusion | flops 2316000 | bytes 4632000 | tf_op jit(solution)/shard_map/concatenate | solution.py:17
  52.8 3.2 %pad_maximum_fusion.24 = (f32[6,50,386]{2,1,0:T(8,128)}, f32[6,50,386]{2,1,0:T(8,128)}) fusion(f32[42,50,1]{2,1,0:T(8,128)S(1)} %copy.100, f32[42,50,1]{2,1,0:T(8,128)} %copy.99, f32[42,1,384]{2,1,0:T(1,128)S(1)} %collective-permute-done.5, f32[42,1,384]{2,1,0:T(1,128)} %copy-done.14, f32[6,48,384]{2,1,0:T(8,128)} %param.9, f32[6,48,384]{2,1,0:T(8,128)} %param.8, ...), kind=kLoop, calls=%fused_computation.68 | loop fusion | flops 1389600 | bytes 4168800 | tf_op jit(solution)/shard_map/slice | solution.py:63
  56.1 2.9 %pad_maximum_fusion = f32[30,50,386]{2,1,0:T(8,128)S(1)} fusion(f32[42,50,1]{2,1,0:T(8,128)} %copy-done.5, f32[42,50,1]{2,1,0:T(8,128)S(1)} %copy-done.6, f32[42,1,384]{2,1,0:T(1,128)S(1)} %collective-permute-done.5, f32[42,1,384]{2,1,0:T(1,128)S(1)} %copy-done.15, f32[6,48,384]{2,1,0:T(8,128)S(1)} %copy-done.10, f32[6,48,384]{2,1,0:T(8,128)S(1)} %copy-done.12, ...), kind=kLoop, calls=%fused_computation | loop fusion | flops 3474000 | bytes 5558400 | tf_op jit(solution)/shard_map/concatenate | solution.py:17
  59.1 2.9 %broadcast_multiply_fusion.5 = (f32[5,6,50,386]{3,2,1,0:T(8,128)S(1)}, f32[5,6,50,386]{3,2,1,0:T(8,128)S(1)}, f32[5,6,50,386]{3,2,1,0:T(8,128)S(1)}) fusion(f32[5,6,50,386]{3,2,1,0:T(8,128)S(1)} %bitcast.48, f32[6,50,386]{2,1,0:T(8,128)} %get-tuple-element.4, f32[5,6,50,386]{3,2,1,0:T(8,128)S(1)} %bitcast.41, f32[6,50,386]{2,1,0:T(8,128)} %get-tuple-element.5), kind=kLoop, calls=%fused_computation.50 | loop fusion | flops 1737000 | bytes 12506400 | tf_op jit(solution)/shard_map/mul | solution.py:29
  62.0 5.2 %fusion.10 = f32[5,6,48,384]{3,2,1,0:T(8,128)S(1)} fusion(f32[5,6,50,386]{3,2,1,0:T(8,128)S(1)} %get-tuple-element.13, f32[5,6,50,386]{3,2,1,0:T(8,128)S(1)} %get-tuple-element.14, f32[5,6,50,386]{3,2,1,0:T(8,128)S(1)} %get-tuple-element.12, f32[5,6,50,386]{3,2,1,0:T(8,128)S(1)} %bitcast.49), kind=kLoop, calls=%fused_computation.34 | loop fusion | flops 6635520 | bytes 24330240 | tf_op jit(solution)/shard_map/sub | solution.py:37
  71.3 3.5 %collective-permute-start.8 = (f32[30,1,384]{2,1,0:T(1,128)}, f32[30,1,384]{2,1,0:T(1,128)S(1)}, u32[]{:S(2)}, u32[]{:S(2)}) collective-permute-start(f32[30,1,384]{2,1,0:T(1,128)} %get-tuple-element.27), channel_id=1, source_target_pairs={{0,8},{8,16},{16,24},{1,9},{9,17},{17,25},{2,10},{10,18},{18,26},{... | collective-permute-start | bytes 138248 | tf_op jit(solution)/shard_map/ppermute | solution.py:19
  76.8 2.9 %pad_maximum_fusion.19 = (f32[30,50,1]{2,1,0:T(8,128)}, f32[30,50,1]{2,1,0:T(8,128)}) fusion(f32[30,1,384]{2,1,0:T(1,128)S(1)} %collective-permute-done.9, f32[30,48,384]{2,1,0:T(8,128)} %bitcast.55, f32[30,1,384]{2,1,0:T(1,128)S(1)} %collective-permute-done.8), kind=kLoop, calls=%fused_computation.63 | loop fusion | flops 6000 | bytes 2316000 | tf_op jit(solution)/shard_map/slice | solution.py:16
  84.8 5.5 %collective-permute-start.10 = (f32[30,50,1]{1,2,0:T(1,128)}, f32[30,50,1]{1,2,0:T(1,128)}, u32[]{:S(2)}, u32[]{:S(2)}) collective-permute-start(f32[30,50,1]{1,2,0:T(1,128)} %copy.101), channel_id=1, source_target_pairs={{0,1},{1,2},{2,3},{3,4},{4,5},{5,6},{6,7},{8,9},{9,10},{10,11},{11... | collective-permute-start | bytes 18008 | tf_op jit(solution)/shard_map/ppermute | solution.py:19
  97.4 3.7 %pad_maximum_fusion.7 = f32[30,50,386]{2,1,0:T(8,128)S(1)} fusion(f32[30,50,1]{2,1,0:T(8,128)} %copy.104, f32[30,1,384]{2,1,0:T(1,128)S(1)} %collective-permute-done.9, f32[30,48,384]{2,1,0:T(8,128)} %bitcast.56, f32[30,1,384]{2,1,0:T(1,128)S(1)} %collective-permute-done.8, f32[30,50,1]{2,1,0:T(8,128)} %copy.103), kind=kLoop, calls=%fused_computation.7 | loop fusion | flops 2316000 | bytes 4632000 | tf_op jit(solution)/shard_map/concatenate | solution.py:17
  104.0 5.2 %fusion.5 = f32[5,6,48,384]{3,2,1,0:T(8,128)S(1)} fusion(f32[5,6,50,386]{3,2,1,0:T(8,128)S(1)} %get-tuple-element.10, f32[5,6,50,386]{3,2,1,0:T(8,128)S(1)} %get-tuple-element.11, f32[5,6,50,386]{3,2,1,0:T(8,128)S(1)} %get-tuple-element.9, f32[5,6,50,386]{3,2,1,0:T(8,128)S(1)} %bitcast.53), kind=kLoop, calls=%fused_computation.22 | loop fusion | flops 6635520 | bytes 24330240 | tf_op jit(solution)/shard_map/sub | solution.py:37
  111.2 3.8 %collective-permute-start.12 = (f32[30,1,384]{2,1,0:T(1,128)S(1)}, f32[30,1,384]{2,1,0:T(1,128)S(1)}, u32[]{:S(2)}, u32[]{:S(2)}) collective-permute-start(f32[30,1,384]{2,1,0:T(1,128)S(1)} %get-tuple-element.25), channel_id=1, source_target_pairs={{0,8},{8,16},{16,24},{1,9},{9,17},{17,25},{2,10},{10,18},{18,26},{... | collective-permute-start | bytes 138248 | tf_op jit(solution)/shard_map/ppermute | solution.py:19
  122.8 5.0 %collective-permute-start.14 = (f32[30,50,1]{1,2,0:T(1,128)}, f32[30,50,1]{1,2,0:T(1,128)}, u32[]{:S(2)}, u32[]{:S(2)}) collective-permute-start(f32[30,50,1]{1,2,0:T(1,128)} %copy.105), channel_id=1, source_target_pairs={{0,1},{1,2},{2,3},{3,4},{4,5},{5,6},{6,7},{8,9},{9,10},{10,11},{11... | collective-permute-start | bytes 18008 | tf_op jit(solution)/shard_map/ppermute | solution.py:19
  131.8 3.7 %pad_maximum_fusion.8 = f32[30,50,386]{2,1,0:T(8,128)S(1)} fusion(f32[30,50,1]{2,1,0:T(8,128)} %copy.108, f32[30,1,384]{2,1,0:T(1,128)} %copy-done.16, f32[30,48,384]{2,1,0:T(8,128)} %bitcast.59, f32[30,1,384]{2,1,0:T(1,128)} %copy-done.17, f32[30,50,1]{2,1,0:T(8,128)} %copy.107), kind=kLoop, calls=%fused_computation.8 | loop fusion | flops 2316000 | bytes 4632000 | tf_op jit(solution)/shard_map/concatenate | solution.py:17
  138.4 6.4 %broadcast_multiply_fusion.6 = (f32[5,6,48,384]{3,2,1,0:T(8,128)S(1)}, f32[5,6,48,384]{3,2,1,0:T(8,128)}) fusion(f32[48,384]{1,0:T(8,128)S(1)} %get-tuple-element.32, f32[5,6,50,386]{3,2,1,0:T(8,128)S(1)} %get-tuple-element.7, f32[5,6,50,386]{3,2,1,0:T(8,128)S(1)} %get-tuple-element.8, f32[5,6,50,386]{3,2,1,0:T(8,128)S(1)} %get-tuple-element.6, ...), kind=kLoop, calls=%fused_computation.56 | loop fusion | flops 7188480 | bytes 26615808 | tf_op jit(solution)/shard_map/mul | solution.py:84
  144.8 30.3 %copy.109 = f32[5,6,48,384]{1,0,3,2:T(8,128)} copy(f32[5,6,48,384]{3,2,1,0:T(8,128)S(1)} %get-tuple-element.2) | data formatting | bytes 4423680 | tf_op jit(solution)/shard_map/mul | solution.py:84
  175.1 49.8 %reshape.185 = f32[30,16,3,128,3]{0,4,3,2,1:T(4,128)} reshape(f32[5,6,48,384]{1,0,3,2:T(8,128)} %copy.109) | data formatting | bytes 4423680 | tf_op jit(solution)/shard_map/reshape | solution.py:84
  224.9 9.1 %reduce_sum.19 = f32[30,16,128]{0,2,1:T(8,128)S(1)} reduce(f32[30,16,3,128,3]{0,4,3,2,1:T(4,128)} %reshape.185, f32[]{:T(128)} %constant.38.clone.1), dimensions={2,4}, to_apply=%region_1.0 | reduce | flops 491520 | bytes 2457604 | tf_op jit(solution)/shard_map/reduce_sum | solution.py:84
  235.5 5.4 %all-to-all-start = ((f32[8,2,30,128]{3,1,2,0:T(2,128)}), f32[8,2,30,128]{3,1,2,0:T(2,128)S(1)}, u32[]{:S(2)}, u32[]{:S(2)}) async-start(f32[8,2,30,128]{3,1,2,0:T(2,128)} %copy.111), calls=%async_computation | async-start | bytes 491520 | tf_op jit(solution)/shard_map/all_to_all | solution.py:104
  245.3 3.8 %all-to-all-done = f32[8,2,30,128]{3,1,2,0:T(2,128)S(1)} async-done(((f32[8,2,30,128]{3,1,2,0:T(2,128)}), f32[8,2,30,128]{3,1,2,0:T(2,128)S(1)}, u32[]{:S(2)}, u32[]{:S(2)}) %all-to-all-start) | async-done | bytes 245792 | tf_op jit(solution)/shard_map/all_to_all | solution.py:104
  (121 shorter events, 68.3 us)
Async XLA Ops:
  0.6 15.0 %copy-start.7 = (f32[5,6,48,384]{3,2,1,0:T(8,128)S(1)}, f32[5,6,48,384]{3,2,1,0:T(8,128)}, u32[]{:S(2)}) copy-start(f32[5,6,48,384]{3,2,1,0:T(8,128)} %param.7) | copy-start | bytes 6635524
  0.6 14.7 %copy-start.24 = (s32[1,16,1]{1,2,0:T(1,128)S(1)}, s32[1,16,1]{1,2,0:T(1,128)}, u32[]{:S(2)}) copy-start(s32[1,16,1]{1,2,0:T(1,128)} %param.12) | copy-start | bytes 196
  2.0 13.6 %collective-permute-start.1 = (f32[30,1,384]{2,1,0:T(1,128)S(1)}, f32[30,1,384]{2,1,0:T(1,128)S(1)}, u32[]{:S(2)}, u32[]{:S(2)}) collective-permute-start(f32[30,1,384]{2,1,0:T(1,128)S(1)} %get-tuple-element.30), channel_id=1, source_target_pairs={{8,0},{16,8},{24,16},{9,1},{17,9},{25,17},{10,2},{18,10},{26,18},{... | collective-permute-start | bytes 138248 | tf_op jit(solution)/shard_map/ppermute | solution.py:21
  3.9 11.7 %collective-permute-start = (f32[30,1,384]{2,1,0:T(1,128)S(1)}, f32[30,1,384]{2,1,0:T(1,128)S(1)}, u32[]{:S(2)}, u32[]{:S(2)}) collective-permute-start(f32[30,1,384]{2,1,0:T(1,128)S(1)} %get-tuple-element.29), channel_id=1, source_target_pairs={{0,8},{8,16},{16,24},{1,9},{9,17},{17,25},{2,10},{10,18},{18,26},{... | collective-permute-start | bytes 138248 | tf_op jit(solution)/shard_map/ppermute | solution.py:19
  9.8 24.9 %collective-permute-start.5 = (f32[42,1,384]{2,1,0:T(1,128)S(1)}, f32[42,1,384]{2,1,0:T(1,128)S(1)}, u32[]{:S(2)}, u32[]{:S(2)}) collective-permute-start(f32[42,1,384]{2,1,0:T(1,128)S(1)} %get-tuple-element.18), channel_id=1, source_target_pairs={{8,0},{16,8},{24,16},{9,1},{17,9},{25,17},{10,2},{18,10},{26,18},{... | collective-permute-start | bytes 193544 | tf_op jit(solution)/shard_map/ppermute | solution.py:21
  11.7 22.9 %collective-permute-start.4 = (f32[42,1,384]{2,1,0:T(1,128)S(1)}, f32[42,1,384]{2,1,0:T(1,128)S(1)}, u32[]{:S(2)}, u32[]{:S(2)}) collective-permute-start(f32[42,1,384]{2,1,0:T(1,128)S(1)} %get-tuple-element.17), channel_id=1, source_target_pairs={{0,8},{8,16},{16,24},{1,9},{9,17},{17,25},{2,10},{10,18},{18,26},{... | collective-permute-start | bytes 193544 | tf_op jit(solution)/shard_map/ppermute | solution.py:19
  17.2 17.5 %copy-start = (f32[5,6,48,384]{3,2,1,0:T(8,128)S(1)}, f32[5,6,48,384]{3,2,1,0:T(8,128)}, u32[]{:S(2)}) copy-start(f32[5,6,48,384]{3,2,1,0:T(8,128)} %param.10) | copy-start | bytes 6635524
  17.2 17.5 %copy-start.9 = (f32[6,48,384]{2,1,0:T(8,128)S(1)}, f32[6,48,384]{2,1,0:T(8,128)}, u32[]{:S(2)}) copy-start(f32[6,48,384]{2,1,0:T(8,128)} %param.9) | copy-start | bytes 1327108
  17.2 17.5 %copy-start.11 = (f32[6,48,384]{2,1,0:T(8,128)S(1)}, f32[6,48,384]{2,1,0:T(8,128)}, u32[]{:S(2)}) copy-start(f32[6,48,384]{2,1,0:T(8,128)} %param.8) | copy-start | bytes 1327108
  18.8 13.2 %collective-permute-start.3 = (f32[30,50,1]{1,2,0:T(1,128)S(1)}, f32[30,50,1]{1,2,0:T(1,128)S(1)}, u32[]{:S(2)}, u32[]{:S(2)}) collective-permute-start(f32[30,50,1]{1,2,0:T(1,128)S(1)} %copy.94), channel_id=1, source_target_pairs={{1,0},{2,1},{3,2},{4,3},{5,4},{6,5},{7,6},{9,8},{10,9},{11,10},{12... | collective-permute-start | bytes 18008 | tf_op jit(solution)/shard_map/ppermute | solution.py:21
  21.6 11.7 %collective-permute-start.2 = (f32[30,50,1]{1,2,0:T(1,128)S(1)}, f32[30,50,1]{1,2,0:T(1,128)S(1)}, u32[]{:S(2)}, u32[]{:S(2)}) collective-permute-start(f32[30,50,1]{1,2,0:T(1,128)S(1)} %copy.93), channel_id=1, source_target_pairs={{0,1},{1,2},{2,3},{3,4},{4,5},{5,6},{6,7},{8,9},{9,10},{10,11},{11... | collective-permute-start | bytes 18008 | tf_op jit(solution)/shard_map/ppermute | solution.py:19
  26.6 208.9 %all-to-all-start.1 = ((f32[8,1,2]{2,1,0:T(1,128)}), f32[8,1,2]{2,1,0:T(1,128)}, u32[]{:S(2)}, u32[]{:S(2)}) async-start(f32[8,1,2]{2,1,0:T(1,128)} %copy.113), calls=%async_computation.1 | async-start | bytes 8192 | tf_op jit(solution)/shard_map/all_to_all | solution.py:105
  38.5 12.3 %collective-permute-start.7 = (f32[42,50,1]{1,0,2:T(8,128)S(1)}, f32[42,50,1]{1,0,2:T(8,128)S(1)}, u32[]{:S(2)}, u32[]{:S(2)}) collective-permute-start(f32[42,50,1]{1,0,2:T(8,128)S(1)} %copy.98), channel_id=1, source_target_pairs={{1,0},{2,1},{3,2},{4,3},{5,4},{6,5},{7,6},{9,8},{10,9},{11,10},{12... | collective-permute-start | bytes 25208 | tf_op jit(solution)/shard_map/ppermute | solution.py:21
  41.6 9.7 %collective-permute-start.6 = (f32[42,50,1]{1,0,2:T(8,128)S(1)}, f32[42,50,1]{1,0,2:T(8,128)S(1)}, u32[]{:S(2)}, u32[]{:S(2)}) collective-permute-start(f32[42,50,1]{1,0,2:T(8,128)S(1)} %copy.97), channel_id=1, source_target_pairs={{0,1},{1,2},{2,3},{3,4},{4,5},{5,6},{6,7},{8,9},{9,10},{10,11},{11... | collective-permute-start | bytes 25208 | tf_op jit(solution)/shard_map/ppermute | solution.py:19
  62.0 12.8 %copy-start.19 = (s32[4]{0:T(128)S(1)}, s32[4]{0:T(128)}, u32[]{:S(2)}) copy-start(s32[4]{0:T(128)} %param.11) | copy-start | bytes 52
  69.2 7.6 %collective-permute-start.9 = (f32[30,1,384]{2,1,0:T(1,128)}, f32[30,1,384]{2,1,0:T(1,128)S(1)}, u32[]{:S(2)}, u32[]{:S(2)}) collective-permute-start(f32[30,1,384]{2,1,0:T(1,128)} %get-tuple-element.28), channel_id=1, source_target_pairs={{8,0},{16,8},{24,16},{9,1},{17,9},{25,17},{10,2},{18,10},{26,18},{... | collective-permute-start | bytes 138248 | tf_op jit(solution)/shard_map/ppermute | solution.py:21
  71.3 5.5 %collective-permute-start.8 = (f32[30,1,384]{2,1,0:T(1,128)}, f32[30,1,384]{2,1,0:T(1,128)S(1)}, u32[]{:S(2)}, u32[]{:S(2)}) collective-permute-start(f32[30,1,384]{2,1,0:T(1,128)} %get-tuple-element.27), channel_id=1, source_target_pairs={{0,8},{8,16},{16,24},{1,9},{9,17},{17,25},{2,10},{10,18},{18,26},{... | collective-permute-start | bytes 138248 | tf_op jit(solution)/shard_map/ppermute | solution.py:19
  81.2 12.2 %collective-permute-start.11 = (f32[30,50,1]{1,2,0:T(1,128)S(1)}, f32[30,50,1]{1,2,0:T(1,128)}, u32[]{:S(2)}, u32[]{:S(2)}) collective-permute-start(f32[30,50,1]{1,2,0:T(1,128)S(1)} %copy.102), channel_id=1, source_target_pairs={{1,0},{2,1},{3,2},{4,3},{5,4},{6,5},{7,6},{9,8},{10,9},{11,10},{12... | collective-permute-start | bytes 18008 | tf_op jit(solution)/shard_map/ppermute | solution.py:21
  84.8 10.6 %collective-permute-start.10 = (f32[30,50,1]{1,2,0:T(1,128)}, f32[30,50,1]{1,2,0:T(1,128)}, u32[]{:S(2)}, u32[]{:S(2)}) collective-permute-start(f32[30,50,1]{1,2,0:T(1,128)} %copy.101), channel_id=1, source_target_pairs={{0,1},{1,2},{2,3},{3,4},{4,5},{5,6},{6,7},{8,9},{9,10},{10,11},{11... | collective-permute-start | bytes 18008 | tf_op jit(solution)/shard_map/ppermute | solution.py:19
  109.2 7.0 %collective-permute-start.13 = (f32[30,1,384]{2,1,0:T(1,128)S(1)}, f32[30,1,384]{2,1,0:T(1,128)S(1)}, u32[]{:S(2)}, u32[]{:S(2)}) collective-permute-start(f32[30,1,384]{2,1,0:T(1,128)S(1)} %get-tuple-element.26), channel_id=1, source_target_pairs={{8,0},{16,8},{24,16},{9,1},{17,9},{25,17},{10,2},{18,10},{26,18},{... | collective-permute-start | bytes 138248 | tf_op jit(solution)/shard_map/ppermute | solution.py:21
  111.2 5.1 %collective-permute-start.12 = (f32[30,1,384]{2,1,0:T(1,128)S(1)}, f32[30,1,384]{2,1,0:T(1,128)S(1)}, u32[]{:S(2)}, u32[]{:S(2)}) collective-permute-start(f32[30,1,384]{2,1,0:T(1,128)S(1)} %get-tuple-element.25), channel_id=1, source_target_pairs={{0,8},{8,16},{16,24},{1,9},{9,17},{17,25},{2,10},{10,18},{18,26},{... | collective-permute-start | bytes 138248 | tf_op jit(solution)/shard_map/ppermute | solution.py:19
  119.3 9.1 %collective-permute-start.15 = (f32[30,50,1]{1,2,0:T(1,128)S(1)}, f32[30,50,1]{1,2,0:T(1,128)S(1)}, u32[]{:S(2)}, u32[]{:S(2)}) collective-permute-start(f32[30,50,1]{1,2,0:T(1,128)S(1)} %copy.106), channel_id=1, source_target_pairs={{1,0},{2,1},{3,2},{4,3},{5,4},{6,5},{7,6},{9,8},{10,9},{11,10},{12... | collective-permute-start | bytes 18008 | tf_op jit(solution)/shard_map/ppermute | solution.py:21
  122.8 7.0 %collective-permute-start.14 = (f32[30,50,1]{1,2,0:T(1,128)}, f32[30,50,1]{1,2,0:T(1,128)}, u32[]{:S(2)}, u32[]{:S(2)}) collective-permute-start(f32[30,50,1]{1,2,0:T(1,128)} %copy.105), channel_id=1, source_target_pairs={{0,1},{1,2},{2,3},{3,4},{4,5},{5,6},{6,7},{8,9},{9,10},{10,11},{11... | collective-permute-start | bytes 18008 | tf_op jit(solution)/shard_map/ppermute | solution.py:19
  235.5 13.6 %all-to-all-start = ((f32[8,2,30,128]{3,1,2,0:T(2,128)}), f32[8,2,30,128]{3,1,2,0:T(2,128)S(1)}, u32[]{:S(2)}, u32[]{:S(2)}) async-start(f32[8,2,30,128]{3,1,2,0:T(2,128)} %copy.111), calls=%async_computation | async-start | bytes 491520 | tf_op jit(solution)/shard_map/all_to_all | solution.py:104
  (20 other events, 113.0 us)
where the time goes:
time: 254 us; the launch traced here: 251 us
  local copies, waits for them, and re-layouts  113 us (44%)
  other arithmetic  70.1 us (28%)
  starting transfers between devices  58 us (23%)
  waiting for transfers between devices  3.81 us (2%)
  between operations  3.72 us (1%)
    reshape x1, local copies, waits for them, and re-layouts, shards(): (weighting * field_now).reshape(planes, coarse_rows, 3, coarse_cols, 3)  49.8 us
    ppermute x8, starting transfers between devices, with_halo(): lax.ppermute(tail, axis, [(i, (i + 1) % count) for i in range(ends)])  33.9 us
    mul x1, local copies, waits for them, and re-layouts, shards(): weighting * field_now  30.3 us
    concatenate x4, other arithmetic, with_halo(): jnp.concatenate([lax.ppermute(tail, axis, [(i, (i + 1) % count) for i in...  15.4 us
    ppermute x8, starting transfers between devices, with_halo(): lax.ppermute(head, axis, [((i + 1) % count, i) for i in range(ends)])  13.2 us
    sub x2, other arithmetic, advance(): return result - 4.0 * spread[..., 1:-1, 1:-1]  10.3 us
    slice x7, local copies, waits for them, and re-layouts, with_halo(): lax.slice_in_dim(cells, cells.shape[dim] - width, cells.shape[dim], axis=...  9.59 us
    slice x5, other arithmetic, with_halo(): lax.slice_in_dim(cells, cells.shape[dim] - width, cells.shape[dim], axis=...  9.3 us
  transfers between devices with their start and end apart: 18, of which 1 were waited for; matrix products, arithmetic and copies ran while one was open for 72% of the time, Pallas kernels for 0%

commit v1 on v0

v1 whole, which is shorter than its diff:
```python
import functools

import jax
import jax.numpy as jnp
from jax import lax
from jax.experimental import pallas as pl
from jax.experimental.pallas import tpu as pltpu
from jax.sharding import PartitionSpec as P

ITERS = 3
PROWS = 80
CAP = 2
LANES = 128
SUB = 8
PACK = 4
MESH = pl.DeviceIdType.MESH
DIRS = ((-1, 0), (1, 0), (0, 1), (0, -1), (-1, 1), (-1, -1), (1, 1), (1, -1))
NORTH, SOUTH, EAST, WEST, NE, NW, SE, SW = range(8)
OPPOSITE = (SOUTH, NORTH, WEST, EAST, SW, SE, NW, NE)


def round_up(value, step):
    return -(-value // step) * step


def split_dot(values, weights):
    high = values.astype(jnp.bfloat16)
    low = (values - high.astype(jnp.float32)).astype(jnp.bfloat16)
    return jnp.dot(high, weights, preferred_element_type=jnp.float32) + jnp.dot(
        low, weights, preferred_element_type=jnp.float32
    )


def kernel(
    dims,
    zone_ref,
    dest_ref,
    slot_ref,
    field_hbm,
    spread_hbm,
    along_x_hbm,
    along_y_hbm,
    nest_hbm,
    parent_ref,
    field,
    spread,
    along_x,
    along_y,
    nest,
    halo,
    keep,
    weigh,
    coarse,
    rows_n,
    rows_s,
    got_n,
    got_s,
    slab_e,
    slab_w,
    got_e,
    got_w,
    got_corner,
    outbound,
    arrived,
    load_sem,
    store_sem,
    send_sem,
    recv_sem,
    out_sem,
    in_sem,
):
    fields, levels, tile_rows, tiles = dims
    planes = fields * levels
    spread_at = round_up(planes, SUB)
    x_at = 2 * spread_at
    y_at = x_at + round_up(levels, SUB)
    total = y_at + round_up(levels, SUB)
    planes_pad = spread_at
    row, col = lax.axis_index("row"), lax.axis_index("col")
    nrow, ncol = lax.axis_size("row"), lax.axis_size("col")
    wide = tile_rows + SUB

    def exists(way):
        down, over = DIRS[way]
        conditions = []
        if down < 0:
            conditions.append(row > 0)
        if down > 0:
            conditions.append(row < nrow - 1)
        if over < 0:
            conditions.append(col > 0)
        if over > 0:
            conditions.append(col < ncol - 1)
        return functools.reduce(jnp.logical_and, conditions)

    def device(way):
        return (row + DIRS[way][0], col + DIRS[way][1])

    barrier = pltpu.get_barrier_semaphore()
    for way in (NORTH, SOUTH, NE, NW, SE, SW):

        @pl.when(exists(way))
        def _(way=way):
            pl.semaphore_signal(barrier, inc=1, device_id=device(way), device_id_type=MESH)

    for step in range(1, ncol):
        pl.semaphore_signal(
            barrier, inc=1, device_id=(row, lax.rem(col + step, ncol)), device_id_type=MESH
        )

    loads = []
    for kind, (source, target) in enumerate(
        ((field_hbm, field), (spread_hbm, spread), (along_x_hbm, along_x), (along_y_hbm, along_y))
    ):
        count = source.shape[0]
        for t in range(tiles):
            copy = pltpu.make_async_copy(
                source.at[:, t * LANES : (t + 1) * LANES],
                target.at[t, 0:count, :],
                load_sem.at[kind * tiles + t],
            )
            copy.start()
            loads.append(copy)

    row_index = row * tile_rows + lax.broadcasted_iota(jnp.int32, (tile_rows, LANES), 0)
    lane = lax.broadcasted_iota(jnp.int32, (tile_rows, LANES), 1)
    grid_rows, grid_cols = tile_rows * nrow, tiles * LANES * ncol

    def ramp(position, count, low_zone, high_zone):
        scale_low = jnp.full((tile_rows, LANES), (low_zone + 1).astype(jnp.float32))
        scale_high = jnp.full((tile_rows, LANES), (high_zone + 1).astype(jnp.float32))
        lower = jnp.maximum(low_zone - position, 0).astype(jnp.float32) / scale_low
        upper = jnp.maximum(high_zone - (count - 1 - position), 0).astype(jnp.float32) / scale_high
        return jnp.maximum(lower, upper)

    weight_rows = ramp(row_index, grid_rows, zone_ref[0], zone_ref[1])
    for t in range(tiles):
        weight_cols = ramp((col * tiles + t) * LANES + lane, grid_cols, zone_ref[2], zone_ref[3])
        relaxation = jnp.maximum(weight_rows, weight_cols)
        keep[t] = 1.0 - relaxation
        weigh[t] = (1.0 - relaxation) / 9.0 + relaxation
    halo[...] = jnp.zeros_like(halo)
    for t in range(tiles):
        extra = (planes_pad - planes) * tile_rows
        if extra:
            field[t, planes * tile_rows :, :] = jnp.zeros((extra, LANES), jnp.float32)

    received = {NORTH: got_n, SOUTH: got_s, EAST: got_e, WEST: got_w}
    for place, way in enumerate((NE, NW, SE, SW)):
        received[way] = got_corner.at[place]
    for way in range(8):

        @pl.when(jnp.logical_not(exists(way)))
        def _(way=way):
            received[way][...] = jnp.zeros(received[way].shape, jnp.float32)

    for copy in loads:
        copy.wait()

    for kind, pieces in enumerate(
        (((field, planes, 0),), ((spread, planes, 0),), ((along_x, levels, 0), (along_y, levels, 8)))
    ):
        first = jnp.zeros((tile_rows, LANES), jnp.float32)
        last = jnp.zeros((tile_rows, LANES), jnp.float32)
        for source, count, base in pieces:

            def pack(p, carry, source=source, base=base):
                first, last = carry
                at = pl.multiple_of(p * tile_rows, SUB)
                here = lane // PACK == p + base
                moved_first = pltpu.roll(source[0, pl.ds(at, tile_rows), :], PACK * (p + base), 1)
                moved_last = pltpu.roll(
                    source[tiles - 1, pl.ds(at, tile_rows), :], PACK * (p + base + 1), 1
                )
                return jnp.where(here, moved_first, first), jnp.where(here, moved_last, last)

            first, last = lax.fori_loop(0, count, pack, (first, last))
        slab_w[kind] = first
        slab_e[kind] = last

    for r in range(ITERS):
        for t in range(tiles):
            for source, count, base in (
                (field, planes, 0),
                (spread, planes, spread_at),
                (along_x, levels, x_at),
                (along_y, levels, y_at),
            ):
                rows_n[r * tiles + t, base : base + count, :] = source[
                    t, pl.ds(r, count, stride=tile_rows), :
                ]
                rows_s[r * tiles + t, base : base + count, :] = source[
                    t, pl.ds(tile_rows - ITERS + r, count, stride=tile_rows), :
                ]

    top, bottom = slice(0, SUB), slice(tile_rows - SUB, tile_rows)
    sources = {
        NORTH: rows_n,
        SOUTH: rows_s,
        EAST: slab_e,
        WEST: slab_w,
        NE: slab_e.at[:, top, :],
        NW: slab_w.at[:, top, :],
        SE: slab_e.at[:, bottom, :],
        SW: slab_w.at[:, bottom, :],
    }

    def remote(way):
        back = OPPOSITE[way]
        return pltpu.make_async_remote_copy(
            src_ref=sources[way],
            dst_ref=received[back],
            send_sem=send_sem.at[way],
            recv_sem=recv_sem.at[back],
            device_id=device(way),
            device_id_type=MESH,
        )

    greeted = jnp.int32(ncol - 1)
    for way in (NORTH, SOUTH, NE, NW, SE, SW):
        greeted = greeted + exists(way).astype(jnp.int32)
    pl.semaphore_wait(barrier, greeted)

    for way in range(8):

        @pl.when(exists(way))
        def _(way=way):
            remote(way).start()

    for way in range(8):

        @pl.when(exists(way))
        def _(way=way):
            pltpu.make_async_remote_copy(
                src_ref=sources[OPPOSITE[way]],
                dst_ref=received[way],
                send_sem=send_sem.at[OPPOSITE[way]],
                recv_sem=recv_sem.at[way],
                device_id=device(way),
                device_id_type=MESH,
            ).wait_recv()

    for r in range(ITERS):
        for t in range(tiles):
            halo[t, pl.ds(r, total, stride=SUB), :] = got_s[r * tiles + t]
            halo[t, pl.ds(SUB - ITERS + r, total, stride=SUB), :] = got_n[r * tiles + t]

    lane_wide = lax.broadcasted_iota(jnp.int32, (wide, LANES), 1)
    lane_low = lax.broadcasted_iota(jnp.int32, (SUB, LANES), 1)
    south_half = lax.broadcasted_iota(jnp.int32, (SUB, LANES), 0) < SUB // 2

    def block(source, p, kind, place, base):
        at = pl.multiple_of(p * tile_rows, SUB)
        low = pl.multiple_of((p + base) * SUB, SUB)
        parts = [
            jnp.concatenate([source[t, pl.ds(at, tile_rows), :], halo[t, pl.ds(low, SUB), :]], 0)
            for t in range(tiles)
        ]
        east = jnp.concatenate(
            [got_e[kind], jnp.where(south_half, got_corner[2, kind], got_corner[0, kind])], 0
        )
        west = jnp.concatenate(
            [got_w[kind], jnp.where(south_half, got_corner[3, kind], got_corner[1, kind])], 0
        )
        east = pltpu.roll(east, lax.rem(LANES - PACK * place, LANES), 1)
        west = pltpu.roll(west, LANES - PACK * (place + 1), 1)
        return parts + [jnp.where(lane_wide < LANES // 2, east, west)]

    span = tiles + 1

    def one_level(level, _):
        half_x = [0.5 * part for part in block(along_x, level, 2, level, x_at)]
        half_y = [0.5 * part for part in block(along_y, level, 2, level + 8, y_at)]

        def one_field(f, _):
            p = f * levels + level
            now = block(field, p, 0, p, 0)
            d = block(spread, p, 1, p, spread_at)
            for sweep in range(ITERS):
                done = tiles if sweep == ITERS - 1 else span
                right = [
                    pltpu.roll(now[t] * (d[t] + half_y[t]), LANES - 1, 1) for t in range(span)
                ]
                left = [pltpu.roll(now[t] * (d[t] - half_y[t]), 1, 1) for t in range(span)]
                later = []
                for t in range(done):
                    value = now[t] * (1.0 - 4.0 * d[t])
                    value = value + pltpu.roll(now[t] * (d[t] + half_x[t]), wide - 1, 0)
                    value = value + pltpu.roll(now[t] * (d[t] - half_x[t]), 1, 0)
                    value = value + jnp.where(
                        lane_wide == LANES - 1, right[(t + 1) % span], right[t]
                    )
                    value = value + jnp.where(lane_wide == 0, left[(t - 1) % span], left[t])
                    later.append(value)
                now = later
            at = pl.multiple_of(p * tile_rows, SUB)
            for t in range(tiles):
                final = now[t][:tile_rows]
                nest[t, pl.ds(at, tile_rows), :] = keep[t] * final
                field[t, pl.ds(at, tile_rows), :] = weigh[t] * final
            return 0

        return lax.fori_loop(0, fields, one_field, 0)

    lax.fori_loop(0, levels, one_level, 0)

    stores = []
    for t in range(tiles):
        copy = pltpu.make_async_copy(
            nest.at[t], nest_hbm.at[:, t * LANES : (t + 1) * LANES], store_sem.at[t]
        )
        copy.start()
        stores.append(copy)

    coarse_rows = tile_rows // 3
    gathered = []
    for t in range(tiles):
        per_row = []
        for g in range(coarse_rows):
            value = field[t, pl.ds(3 * g, planes_pad, stride=tile_rows), :]
            value = value + field[t, pl.ds(3 * g + 1, planes_pad, stride=tile_rows), :]
            value = value + field[t, pl.ds(3 * g + 2, planes_pad, stride=tile_rows), :]
            per_row.append(value)
        gathered.append(jnp.concatenate(per_row, 0))
    sums = None
    for t in range(tiles):
        fine = t * LANES + lax.broadcasted_iota(jnp.int32, (LANES, LANES), 0)
        name = lax.broadcasted_iota(jnp.int32, (LANES, LANES), 1)
        pick = (fine // 3 == name).astype(jnp.float32).astype(jnp.bfloat16)
        term = split_dot(gathered[t], pick)
        sums = term if sums is None else sums + term
    coarse[...] = sums

    dests = [dest_ref[0, g, 0] for g in range(coarse_rows)]
    spots = []
    for g in range(coarse_rows):
        rank = jnp.int32(0)
        for before in range(g):
            rank = rank + jnp.where(dests[before] == dests[g], 1, 0)
        spots.append(dests[g] * CAP + rank)
    tag_row = lax.broadcasted_iota(jnp.int32, (planes_pad, LANES), 0) == planes
    blocks = []
    for g in range(coarse_rows):
        tag = (slot_ref[0, g, 0] + 1).astype(jnp.float32)
        blocks.append(jnp.where(tag_row, tag, coarse[g * planes_pad : (g + 1) * planes_pad, :]))
    for k in range(ncol * CAP):
        value = None
        for g in range(coarse_rows):
            term = jnp.where(spots[g] == k, 1.0, 0.0) * blocks[g]
            value = term if value is None else value + term
        outbound[k // CAP, (k % CAP) * planes_pad : (k % CAP + 1) * planes_pad, :] = value

    arrived[0 : CAP * planes_pad, :] = outbound[col]

    def to_owner(step):
        owner = lax.rem(col + step, ncol)
        return pltpu.make_async_remote_copy(
            src_ref=outbound.at[owner],
            dst_ref=arrived.at[pl.ds(step * CAP * planes_pad, CAP * planes_pad), :],
            send_sem=out_sem.at[step],
            recv_sem=in_sem.at[step],
            device_id=(row, owner),
            device_id_type=MESH,
        )

    for step in range(1, ncol):
        to_owner(step).start()
    for step in range(1, ncol):
        to_owner(step).wait_recv()

    count = ncol * CAP
    tags = arrived[pl.ds(planes, count, stride=planes_pad), :]
    parent_row = lax.broadcasted_iota(jnp.int32, (count, LANES), 1).astype(jnp.float32) + 1.0
    picked = (tags == parent_row).astype(jnp.float32)
    stack = jnp.concatenate(
        [picked, picked, jnp.zeros((LANES - 2 * count, LANES), jnp.float32)], 0
    )
    picker = stack.T[:PROWS].astype(jnp.bfloat16)
    filler = jnp.zeros((LANES - 2 * count, LANES), jnp.bfloat16)
    for p in range(planes):
        value = arrived[pl.ds(p, count, stride=planes_pad), :]
        high = value.astype(jnp.bfloat16)
        low = (value - high.astype(jnp.float32)).astype(jnp.bfloat16)
        parent_ref[p] = jnp.dot(
            picker, jnp.concatenate([high, low, filler], 0), preferred_element_type=jnp.float32
        )

    for way in range(8):

        @pl.when(exists(way))
        def _(way=way):
            remote(way).wait_send()

    for step in range(1, ncol):
        to_owner(step).wait_send()
    for copy in stores:
        copy.wait()


def shards(adjoint_field, advect_x, advect_y, diffusion, zone_cells, feedback_dest, feedback_slot):
    fields, levels, tile_rows, tile_cols = adjoint_field.shape
    planes = fields * levels
    tiles = tile_cols // LANES
    nrow, ncol = lax.axis_size("row"), lax.axis_size("col")
    planes_pad = round_up(planes, SUB)
    levels_pad = round_up(levels, SUB)
    total = 2 * planes_pad + 2 * levels_pad
    own = (tiles, planes_pad * tile_rows, LANES)
    level_own = (tiles, levels * tile_rows, LANES)
    f32 = jnp.float32
    vmem = pltpu.VMEM
    dma = pltpu.SemaphoreType.DMA
    smem_spec = pl.BlockSpec(memory_space=pltpu.SMEM)
    any_spec = pl.BlockSpec(memory_space=pl.ANY)
    nest, parent = pl.pallas_call(
        functools.partial(kernel, (fields, levels, tile_rows, tiles)),
        out_shape=(
            jax.ShapeDtypeStruct((planes * tile_rows, tile_cols), f32),
            jax.ShapeDtypeStruct((planes, PROWS, LANES), f32),
        ),
        in_specs=[smem_spec] * 3 + [any_spec] * 4,
        out_specs=(any_spec, pl.BlockSpec(memory_space=pltpu.VMEM)),
        scratch_shapes=[
            vmem(own, f32),
            vmem((tiles, planes * tile_rows, LANES), f32),
            vmem(level_own, f32),
            vmem(level_own, f32),
            vmem((tiles, planes * tile_rows, LANES), f32),
            vmem((tiles, total * SUB, LANES), f32),
            vmem((tiles, tile_rows, LANES), f32),
            vmem((tiles, tile_rows, LANES), f32),
            vmem((tile_rows // 3 * planes_pad, LANES), f32),
        ]
        + [vmem((ITERS * tiles, total, LANES), f32)] * 4
        + [vmem((3, tile_rows, LANES), f32)] * 4
        + [
            vmem((4, 3, SUB, LANES), f32),
            vmem((ncol, CAP * planes_pad, LANES), f32),
            vmem((ncol * CAP * planes_pad, LANES), f32),
            dma((4 * tiles,)),
            dma((tiles,)),
            dma((8,)),
            dma((8,)),
            dma((ncol,)),
            dma((ncol,)),
        ],
        compiler_params=pltpu.CompilerParams(
            collective_id=0, has_side_effects=True, vmem_limit_bytes=60 * 1024 * 1024
        ),
    )(
        zone_cells,
        feedback_dest,
        feedback_slot,
        adjoint_field.reshape(planes * tile_rows, tile_cols),
        diffusion.reshape(planes * tile_rows, tile_cols),
        advect_x.reshape(levels * tile_rows, tile_cols),
        advect_y.reshape(levels * tile_rows, tile_cols),
    )
    return (
        nest.reshape(adjoint_field.shape),
        parent.reshape(fields, levels, PROWS, LANES),
    )


def solution(mesh):
    placed = (
        P(None, None, "row", "col"),
        P(None, "row", "col"),
        P(None, "row", "col"),
        P(None, None, "row", "col"),
        P(),
        P("col", "row", None),
        P("col", "row", None),
    )
    return jax.shard_map(
        shards,
        mesh=mesh,
        in_specs=placed,
        out_specs=(P(None, None, "row", "col"), P(None, None, "row", "col")),
        check_vma=False,
    )
```

time: 254 us -> 48.8 us (0.19); the launches traced: 251 us -> 48.3 us
  local copies, waits for them, and re-layouts: 113 us -> 6.91 us
  other arithmetic: 70.1 us -> 0 us
  starting transfers between devices: 58 us -> 0 us
  Pallas kernels: 0 us -> 40.8 us
  waiting for transfers between devices: 3.81 us -> 0 us
  between operations: 3.72 us -> 0.65 us
    reshape x1 -> x0, local copies, waits for them, and re-layouts: 49.8 us -> none  [shards(): (weighting * field_now).reshape(planes, coarse_rows, 3, coarse_cols, 3)]
    ppermute x16 -> x0, starting transfers between devices: 47.2 us -> none  [the longest x8 33.9 us: with_halo(): lax.ppermute(tail, axis, [(i, (i + 1) % count) for i in range(ends)])]
    pallas_call x0 -> x1, Pallas kernels: none -> 40.8 us  [shards(): pl.pallas_call(functools.partial(kernel, (fields, levels, tile_rows, tile...]
    mul x1 -> x0, local copies, waits for them, and re-layouts: 30.3 us -> none  [shards(): weighting * field_now]
    mul x5 -> x0, other arithmetic: 17.4 us -> none  [the longest x3 8.62 us: advance(): flux_x = coef_x * widened]
    slice x12 -> x0, local copies, waits for them, and re-layouts: 16.8 us -> none  [the longest x7 9.59 us: with_halo(): lax.slice_in_dim(cells, cells.shape[dim] - width, cells.shape[dim], axis=...]
    concatenate x4 -> x0, other arithmetic: 15.4 us -> none  [with_halo(): jnp.concatenate([lax.ppermute(tail, axis, [(i, (i + 1) % count) for i in...]
    slice x6 -> x0, other arithmetic: 12.5 us -> none  [the longest x5 9.3 us: with_halo(): lax.slice_in_dim(cells, cells.shape[dim] - width, cells.shape[dim], axis=...]
  transfers between devices with their start and end apart: 18 -> 0, of which waited for: 1 -> 0; matrix products, arithmetic and copies ran while one was open for 72% -> 0% of each run, Pallas kernels for 0% -> 0%
where the time goes in v1:
time: 48.8 us; the launch traced here: 48.3 us
  Pallas kernels  40.8 us (84%)
  local copies, waits for them, and re-layouts  6.91 us (14%)
  between operations  0.65 us (1%)
    pallas_call x1, Pallas kernels, shards(): pl.pallas_call(functools.partial(kernel, (fields, levels, tile_rows, tile...  40.8 us
    unnamed x6, local copies, waits for them, and re-layouts  6.91 us

profile of v1, /device:TPU:1, one launch (start us, length us, event | category | flops | bytes accessed | tf_op | source)
XLA Modules:
  0.0 48.3 jit_solution(17040356374857189469)
XLA Ops:
  0.6 1.3 %copy.9.dest_ref = s32[1,16,1]{2,1,0:T(8,128)} copy(s32[1,16,1]{1,2,0:T(1,128)} %param.12) | data formatting | bytes 128 | tf_op args[5]
  2.0 1.3 %copy.10.slot_ref = s32[1,16,1]{2,1,0:T(8,128)} copy(s32[1,16,1]{1,2,0:T(1,128)} %param.13) | data formatting | bytes 128 | tf_op args[6]
  3.3 40.8 %shard_map.86 = (f32[1440,384]{1,0:T(8,128)}, f32[30,80,128]{2,1,0:T(8,128)}) custom-call(s32[4]{0:T(128)} %zone_ref.1, s32[1,16,1]{2,1,0:T(8,128)} %copy.9.dest_ref, s32[1,16,1]{2,1,0:T(8,128)} %copy.10.slot_ref, f32[1440,384]{1,0:T(8,128)} %bitcast.6, f32[1440,384]{1,0:T(8,128)} %bitcast.7, f32[288,384]{1,0:T(8,128)} %bitcast.10, f32[288,384]{1,0:T(8,128)} %bitcast.11), custom_call_target="tpu_custom_call" | custom-call | tf_op jit(solution)/shard_map/pallas_call | solution.py:415
  44.1 0.0 copy-start
  44.1 3.2 %copy.13 = f32[5,6,48,384]{3,2,1,0:T(8,128)} copy(f32[5,6,48,384]{3,2,1,0:T(8,128)} %bitcast.8) | data formatting | bytes 4423680
  47.3 0.0 copy-done
  47.3 1.0 %copy.14 = f32[5,6,80,128]{3,2,1,0:T(8,128)} copy(f32[5,6,80,128]{3,2,1,0:T(8,128)S(1)} %bitcast.9) | data formatting | bytes 2457600
Async XLA Ops:
  44.1 3.2 %copy-start = (f32[30,80,128]{2,1,0:T(8,128)S(1)}, f32[30,80,128]{2,1,0:T(8,128)}, u32[]{:S(2)}) copy-start(f32[30,80,128]{2,1,0:T(8,128)} %get-tuple-element.5) | copy-start | bytes 3686404

commit v2 on v1

--- a/solution.py
+++ b/solution.py
@@ -40,13 +40,12 @@
     spread_hbm,
     along_x_hbm,
     along_y_hbm,
-    nest_hbm,
-    parent_ref,
+    nest,
+    arrived,
     field,
     spread,
     along_x,
     along_y,
-    nest,
     halo,
     keep,
     weigh,
@@ -61,9 +60,7 @@
     got_w,
     got_corner,
     outbound,
-    arrived,
     load_sem,
-    store_sem,
     send_sem,
     recv_sem,
     out_sem,
@@ -174,7 +171,7 @@
                 )
                 return jnp.where(here, moved_first, first), jnp.where(here, moved_last, last)
 
-            first, last = lax.fori_loop(0, count, pack, (first, last))
+            first, last = lax.fori_loop(0, count, pack, (first, last), unroll=6)
         slab_w[kind] = first
         slab_e[kind] = last
 
@@ -304,14 +301,6 @@
 
     lax.fori_loop(0, levels, one_level, 0)
 
-    stores = []
-    for t in range(tiles):
-        copy = pltpu.make_async_copy(
-            nest.at[t], nest_hbm.at[:, t * LANES : (t + 1) * LANES], store_sem.at[t]
-        )
-        copy.start()
-        stores.append(copy)
-
     coarse_rows = tile_rows // 3
     gathered = []
     for t in range(tiles):
@@ -331,7 +320,7 @@
         sums = term if sums is None else sums + term
     coarse[...] = sums
 
-    dests = [dest_ref[0, g, 0] for g in range(coarse_rows)]
+    dests = [dest_ref[g] for g in range(coarse_rows)]
     spots = []
     for g in range(coarse_rows):
         rank = jnp.int32(0)
@@ -341,7 +330,7 @@
     tag_row = lax.broadcasted_iota(jnp.int32, (planes_pad, LANES), 0) == planes
     blocks = []
     for g in range(coarse_rows):
-        tag = (slot_ref[0, g, 0] + 1).astype(jnp.float32)
+        tag = (slot_ref[g] + 1).astype(jnp.float32)
         blocks.append(jnp.where(tag_row, tag, coarse[g * planes_pad : (g + 1) * planes_pad, :]))
     for k in range(ncol * CAP):
         value = None
@@ -368,6 +357,27 @@
     for step in range(1, ncol):
         to_owner(step).wait_recv()
 
+    for way in range(8):
+
+        @pl.when(exists(way))
+        def _(way=way):
+            remote(way).wait_send()
+
+    for step in range(1, ncol):
+        to_owner(step).wait_send()
+
+
+def finish(dims, nest, arrived, nest_hbm, parent_ref, store_sem):
+    planes, tiles, ncol = dims
+    planes_pad = round_up(planes, SUB)
+    stores = []
+    for t in range(tiles):
+        copy = pltpu.make_async_copy(
+            nest.at[t], nest_hbm.at[:, t * LANES : (t + 1) * LANES], store_sem.at[t]
+        )
+        copy.start()
+        stores.append(copy)
+
     count = ncol * CAP
     tags = arrived[pl.ds(planes, count, stride=planes_pad), :]
     parent_row = lax.broadcasted_iota(jnp.int32, (count, LANES), 1).astype(jnp.float32) + 1.0
@@ -385,14 +395,6 @@
             picker, jnp.concatenate([high, low, filler], 0), preferred_element_type=jnp.float32
         )
 
-    for way in range(8):
-
-        @pl.when(exists(way))
-        def _(way=way):
-            remote(way).wait_send()
-
-    for step in range(1, ncol):
-        to_owner(step).wait_send()
     for copy in stores:
         copy.wait()
 
@@ -412,20 +414,19 @@
     dma = pltpu.SemaphoreType.DMA
     smem_spec = pl.BlockSpec(memory_space=pltpu.SMEM)
     any_spec = pl.BlockSpec(memory_space=pl.ANY)
-    nest, parent = pl.pallas_call(
+    nest_shape = (tiles, planes * tile_rows, LANES)
+    arrived_shape = (ncol * CAP * planes_pad, LANES)
+    vmem_spec = pl.BlockSpec(memory_space=pltpu.VMEM)
+    nest, arrived = pl.pallas_call(
         functools.partial(kernel, (fields, levels, tile_rows, tiles)),
-        out_shape=(
-            jax.ShapeDtypeStruct((planes * tile_rows, tile_cols), f32),
-            jax.ShapeDtypeStruct((planes, PROWS, LANES), f32),
-        ),
+        out_shape=(pltpu.VMEM(nest_shape, f32), pltpu.VMEM(arrived_shape, f32)),
         in_specs=[smem_spec] * 3 + [any_spec] * 4,
-        out_specs=(any_spec, pl.BlockSpec(memory_space=pltpu.VMEM)),
+        out_specs=(vmem_spec, vmem_spec),
         scratch_shapes=[
             vmem(own, f32),
             vmem((tiles, planes * tile_rows, LANES), f32),
             vmem(level_own, f32),
             vmem(level_own, f32),
-            vmem((tiles, planes * tile_rows, LANES), f32),
             vmem((tiles, total * SUB, LANES), f32),
             vmem((tiles, tile_rows, LANES), f32),
             vmem((tiles, tile_rows, LANES), f32),
@@ -436,26 +437,35 @@
         + [
             vmem((4, 3, SUB, LANES), f32),
             vmem((ncol, CAP * planes_pad, LANES), f32),
-            vmem((ncol * CAP * planes_pad, LANES), f32),
             dma((4 * tiles,)),
-            dma((tiles,)),
             dma((8,)),
             dma((8,)),
             dma((ncol,)),
             dma((ncol,)),
         ],
         compiler_params=pltpu.CompilerParams(
-            collective_id=0, has_side_effects=True, vmem_limit_bytes=60 * 1024 * 1024
+            collective_id=0, has_side_effects=True, vmem_limit_bytes=61 * 1024 * 1024
         ),
     )(
         zone_cells,
-        feedback_dest,
-        feedback_slot,
+        feedback_dest.reshape(-1),
+        feedback_slot.reshape(-1),
         adjoint_field.reshape(planes * tile_rows, tile_cols),
         diffusion.reshape(planes * tile_rows, tile_cols),
         advect_x.reshape(levels * tile_rows, tile_cols),
         advect_y.reshape(levels * tile_rows, tile_cols),
     )
+    nest, parent = pl.pallas_call(
+        functools.partial(finish, (planes, tiles, ncol)),
+        out_shape=(
+            jax.ShapeDtypeStruct((planes * tile_rows, tile_cols), f32),
+            jax.ShapeDtypeStruct((planes, PROWS, LANES), f32),
+        ),
+        in_specs=[vmem_spec, vmem_spec],
+        out_specs=(any_spec, vmem_spec),
+        scratch_shapes=[dma((tiles,))],
+        compiler_params=pltpu.CompilerParams(vmem_limit_bytes=16 * 1024 * 1024),
+    )(nest, arrived)
     return (
         nest.reshape(adjoint_field.shape),
         parent.reshape(fields, levels, PROWS, LANES),

time: 48.8 us -> 38 us (0.78)
  local copies, waits for them, and re-layouts: 6.91 us -> 0 us
  Pallas kernels: 40.8 us -> 37 us
    unnamed x6 -> x0, local copies, waits for them, and re-layouts: 6.91 us -> none
    pallas_call x1, Pallas kernels: 40.8 us -> 34.5 us  [shards(): pl.pallas_call(functools.partial(kernel, (fields, levels, tile_rows, tile...]
    pallas_call x0 -> x1, Pallas kernels: none -> 2.44 us  [shards(): pl.pallas_call(functools.partial(finish, (planes, tiles, ncol)), out_shap...]
where the time goes in v2:
time: 38 us; the launch traced here: 37.6 us
  Pallas kernels  37 us (97%)
  between operations  0.64 us (2%)
    pallas_call x1, Pallas kernels, shards(): pl.pallas_call(functools.partial(kernel, (fields, levels, tile_rows, tile...  34.5 us
    pallas_call x1, Pallas kernels, shards(): pl.pallas_call(functools.partial(finish, (planes, tiles, ncol)), out_shap...  2.44 us

profile of v2, /device:TPU:1, one launch (start us, length us, event | category | flops | bytes accessed | tf_op | source)
XLA Modules:
  0.0 37.6 jit_solution(9518896621342193176)
XLA Ops:
  0.6 34.5 %shard_map.86 = (f32[3,1440,128]{2,1,0:T(8,128)S(1)}, f32[512,128]{1,0:T(8,128)S(1)}) custom-call(s32[4]{0:T(128)} %zone_ref.1, s32[16]{0:T(128)} %bitcast.12, s32[16]{0:T(128)} %bitcast.13, f32[1440,384]{1,0:T(8,128)} %bitcast.8, f32[1440,384]{1,0:T(8,128)} %bitcast.9, f32[288,384]{1,0:T(8,128)} %bitcast.10, f32[288,384]{1,0:T(8,128)} %bitcast.11), custom_call_target="tpu_custom_call" | custom-call | tf_op jit(solution)/shard_map/pallas_call | solution.py:420
  35.2 2.4 %shard_map.87 = (f32[1440,384]{1,0:T(8,128)}, f32[30,80,128]{2,1,0:T(8,128)}) custom-call(f32[3,1440,128]{2,1,0:T(8,128)S(1)} %get-tuple-element.6.nest, f32[512,128]{1,0:T(8,128)S(1)} %get-tuple-element.7.arrived), custom_call_target="tpu_custom_call" | custom-call | tf_op jit(solution)/shard_map/pallas_call | solution.py:458

commit v3 on v2

--- a/solution.py
+++ b/solution.py
@@ -23,6 +23,15 @@
     return -(-value // step) * step
 
 
+def level_groups(fields, levels):
+    groups, start = [], 0
+    while start < levels:
+        stop = start + -(-(levels - start) // 2)
+        groups.append((start, stop, round_up((stop - start) * fields + 1, SUB)))
+        start = stop
+    return groups
+
+
 def split_dot(values, weights):
     high = values.astype(jnp.bfloat16)
     low = (values - high.astype(jnp.float32)).astype(jnp.bfloat16)
@@ -40,8 +49,12 @@
     spread_hbm,
     along_x_hbm,
     along_y_hbm,
-    nest,
-    arrived,
+    *refs,
+):
+    count_groups = len(level_groups(dims[0], dims[1]))
+    nest, arrived = refs[0], refs[1 : 1 + count_groups]
+    outbound = refs[1 + count_groups : 1 + 2 * count_groups]
+    (
     field,
     spread,
     along_x,
@@ -59,13 +72,15 @@
     got_e,
     got_w,
     got_corner,
-    outbound,
+    got_own,
+    edges,
+    weighted,
     load_sem,
     send_sem,
     recv_sem,
     out_sem,
     in_sem,
-):
+    ) = refs[1 + 2 * count_groups :]
     fields, levels, tile_rows, tiles = dims
     planes = fields * levels
     spread_at = round_up(planes, SUB)
@@ -137,11 +152,6 @@
         keep[t] = 1.0 - relaxation
         weigh[t] = (1.0 - relaxation) / 9.0 + relaxation
     halo[...] = jnp.zeros_like(halo)
-    for t in range(tiles):
-        extra = (planes_pad - planes) * tile_rows
-        if extra:
-            field[t, planes * tile_rows :, :] = jnp.zeros((extra, LANES), jnp.float32)
-
     received = {NORTH: got_n, SOUTH: got_s, EAST: got_e, WEST: got_w}
     for place, way in enumerate((NE, NW, SE, SW)):
         received[way] = got_corner.at[place]
@@ -150,6 +160,10 @@
         @pl.when(jnp.logical_not(exists(way)))
         def _(way=way):
             received[way][...] = jnp.zeros(received[way].shape, jnp.float32)
+            if way in (NORTH, SOUTH):
+                for side in range(2):
+                    shape = got_own.shape[1:]
+                    got_own[2 * side + way] = jnp.zeros(shape, jnp.float32)
 
     for copy in loads:
         copy.wait()
@@ -213,6 +227,20 @@
             device_id_type=MESH,
         )
 
+    def own_columns(way, side, arriving):
+        back = OPPOSITE[way]
+        sent = back if arriving else way
+        place = 2 * side + (way if arriving else back)
+        slab = (slab_e, slab_w)[side]
+        return pltpu.make_async_remote_copy(
+            src_ref=slab.at[:, top if sent == NORTH else bottom, :],
+            dst_ref=got_own.at[place],
+            send_sem=send_sem.at[8 + 2 * side + sent],
+            recv_sem=recv_sem.at[8 + place],
+            device_id=device(way),
+            device_id_type=MESH,
+        )
+
     greeted = jnp.int32(ncol - 1)
     for way in (NORTH, SOUTH, NE, NW, SE, SW):
         greeted = greeted + exists(way).astype(jnp.int32)
@@ -222,6 +250,9 @@
 
         @pl.when(exists(way))
         def _(way=way):
+            if way in (NORTH, SOUTH):
+                for side in range(2):
+                    own_columns(way, side, False).start()
             remote(way).start()
 
     for way in range(8):
@@ -236,6 +267,9 @@
                 device_id=device(way),
                 device_id_type=MESH,
             ).wait_recv()
+            if way in (NORTH, SOUTH):
+                for side in range(2):
+                    own_columns(way, side, True).wait_recv()
 
     for r in range(ITERS):
         for t in range(tiles):
@@ -246,80 +280,103 @@
     lane_low = lax.broadcasted_iota(jnp.int32, (SUB, LANES), 1)
     south_half = lax.broadcasted_iota(jnp.int32, (SUB, LANES), 0) < SUB // 2
 
-    def block(source, p, kind, place, base):
+    def block(source, p, base):
         at = pl.multiple_of(p * tile_rows, SUB)
         low = pl.multiple_of((p + base) * SUB, SUB)
-        parts = [
+        return [
             jnp.concatenate([source[t, pl.ds(at, tile_rows), :], halo[t, pl.ds(low, SUB), :]], 0)
             for t in range(tiles)
         ]
-        east = jnp.concatenate(
-            [got_e[kind], jnp.where(south_half, got_corner[2, kind], got_corner[0, kind])], 0
-        )
-        west = jnp.concatenate(
-            [got_w[kind], jnp.where(south_half, got_corner[3, kind], got_corner[1, kind])], 0
-        )
-        east = pltpu.roll(east, lax.rem(LANES - PACK * place, LANES), 1)
-        west = pltpu.roll(west, LANES - PACK * (place + 1), 1)
-        return parts + [jnp.where(lane_wide < LANES // 2, east, west)]
-
-    span = tiles + 1
+
+    def advance(now, d, half_x, half_y, rights, lefts, count):
+        later = []
+        for t in range(count):
+            value = now[t] * (1.0 - 4.0 * d[t])
+            value = value + pltpu.roll(now[t] * (d[t] + half_x[t]), wide - 1, 0)
+            value = value + pltpu.roll(now[t] * (d[t] - half_x[t]), 1, 0)
+            later.append(value + rights[t] + lefts[t])
+        return later
+
+    def with_rows(slab, kind, from_south, from_north):
+        return jnp.concatenate([slab[kind], jnp.where(south_half, from_south, from_north)], 0)
+
+    period = PACK * levels
+
+    def each_field(slab, base):
+        value = None
+        for f in range(fields):
+            moved = pltpu.roll(slab, (period * f - PACK * base) % LANES, 1)
+            value = moved if value is None else jnp.where(lane_wide >= period * f, moved, value)
+        return value
+
+    inner = lane_wide % PACK
+    for side in range(2):
+        own, other = ((slab_e, got_e), (slab_w, got_w))[side]
+        below, above = ((2, 0), (3, 1))[side]
+        kinds = []
+        for kind in range(3):
+            pair = [
+                with_rows(own, kind, got_own[2 * side + SOUTH, kind], got_own[2 * side + NORTH, kind]),
+                with_rows(other, kind, got_corner[below, kind], got_corner[above, kind]),
+            ]
+            kinds.append(pair if side == 0 else pair[::-1])
+        now, d, along = kinds
+        half_x = [0.5 * each_field(part, 0) for part in along]
+        half_y = [0.5 * each_field(part, 8) for part in along]
+        for sweep in range(ITERS):
+            right = [now[t] * (d[t] + half_y[t]) for t in range(2)]
+            left = [now[t] * (d[t] - half_y[t]) for t in range(2)]
+            edges[side, sweep] = right[1] if side == 0 else left[0]
+            if sweep < ITERS - 1:
+                rights = [
+                    jnp.where(
+                        inner == PACK - 1,
+                        pltpu.roll(right[1], PACK - 1, 1),
+                        pltpu.roll(right[0], LANES - 1, 1),
+                    ),
+                    pltpu.roll(right[1], LANES - 1, 1),
+                ]
+                lefts = [
+                    pltpu.roll(left[0], 1, 1),
+                    jnp.where(
+                        inner == 0,
+                        pltpu.roll(left[0], LANES - PACK + 1, 1),
+                        pltpu.roll(left[1], 1, 1),
+                    ),
+                ]
+                now = advance(now, d, half_x, half_y, rights, lefts, 2)
 
     def one_level(level, _):
-        half_x = [0.5 * part for part in block(along_x, level, 2, level, x_at)]
-        half_y = [0.5 * part for part in block(along_y, level, 2, level + 8, y_at)]
+        half_x = [0.5 * part for part in block(along_x, level, x_at)]
+        half_y = [0.5 * part for part in block(along_y, level, y_at)]
 
         def one_field(f, _):
             p = f * levels + level
-            now = block(field, p, 0, p, 0)
-            d = block(spread, p, 1, p, spread_at)
+            now = block(field, p, 0)
+            d = block(spread, p, spread_at)
             for sweep in range(ITERS):
-                done = tiles if sweep == ITERS - 1 else span
                 right = [
-                    pltpu.roll(now[t] * (d[t] + half_y[t]), LANES - 1, 1) for t in range(span)
+                    pltpu.roll(now[t] * (d[t] + half_y[t]), LANES - 1, 1) for t in range(tiles)
                 ]
-                left = [pltpu.roll(now[t] * (d[t] - half_y[t]), 1, 1) for t in range(span)]
-                later = []
-                for t in range(done):
-                    value = now[t] * (1.0 - 4.0 * d[t])
-                    value = value + pltpu.roll(now[t] * (d[t] + half_x[t]), wide - 1, 0)
-                    value = value + pltpu.roll(now[t] * (d[t] - half_x[t]), 1, 0)
-                    value = value + jnp.where(
-                        lane_wide == LANES - 1, right[(t + 1) % span], right[t]
-                    )
-                    value = value + jnp.where(lane_wide == 0, left[(t - 1) % span], left[t])
-                    later.append(value)
-                now = later
+                left = [pltpu.roll(now[t] * (d[t] - half_y[t]), 1, 1) for t in range(tiles)]
+                right.append(pltpu.roll(edges[0, sweep], LANES - 1 - PACK * p, 1))
+                left.append(pltpu.roll(edges[1, sweep], LANES - PACK + 1 - PACK * p, 1))
+                rights = [
+                    jnp.where(lane_wide == LANES - 1, right[t + 1], right[t]) for t in range(tiles)
+                ]
+                lefts = [jnp.where(lane_wide == 0, left[t - 1], left[t]) for t in range(tiles)]
+                now = advance(now, d, half_x, half_y, rights, lefts, tiles)
             at = pl.multiple_of(p * tile_rows, SUB)
+            to = pl.multiple_of((level * fields + f) * tile_rows, SUB)
             for t in range(tiles):
                 final = now[t][:tile_rows]
                 nest[t, pl.ds(at, tile_rows), :] = keep[t] * final
-                field[t, pl.ds(at, tile_rows), :] = weigh[t] * final
+                weighted[t, pl.ds(to, tile_rows), :] = weigh[t] * final
             return 0
 
         return lax.fori_loop(0, fields, one_field, 0)
 
-    lax.fori_loop(0, levels, one_level, 0)
-
     coarse_rows = tile_rows // 3
-    gathered = []
-    for t in range(tiles):
-        per_row = []
-        for g in range(coarse_rows):
-            value = field[t, pl.ds(3 * g, planes_pad, stride=tile_rows), :]
-            value = value + field[t, pl.ds(3 * g + 1, planes_pad, stride=tile_rows), :]
-            value = value + field[t, pl.ds(3 * g + 2, planes_pad, stride=tile_rows), :]
-            per_row.append(value)
-        gathered.append(jnp.concatenate(per_row, 0))
-    sums = None
-    for t in range(tiles):
-        fine = t * LANES + lax.broadcasted_iota(jnp.int32, (LANES, LANES), 0)
-        name = lax.broadcasted_iota(jnp.int32, (LANES, LANES), 1)
-        pick = (fine // 3 == name).astype(jnp.float32).astype(jnp.bfloat16)
-        term = split_dot(gathered[t], pick)
-        sums = term if sums is None else sums + term
-    coarse[...] = sums
-
     dests = [dest_ref[g] for g in range(coarse_rows)]
     spots = []
     for g in range(coarse_rows):
@@ -327,49 +384,77 @@
         for before in range(g):
             rank = rank + jnp.where(dests[before] == dests[g], 1, 0)
         spots.append(dests[g] * CAP + rank)
-    tag_row = lax.broadcasted_iota(jnp.int32, (planes_pad, LANES), 0) == planes
-    blocks = []
-    for g in range(coarse_rows):
-        tag = (slot_ref[g] + 1).astype(jnp.float32)
-        blocks.append(jnp.where(tag_row, tag, coarse[g * planes_pad : (g + 1) * planes_pad, :]))
-    for k in range(ncol * CAP):
-        value = None
-        for g in range(coarse_rows):
-            term = jnp.where(spots[g] == k, 1.0, 0.0) * blocks[g]
-            value = term if value is None else value + term
-        outbound[k // CAP, (k % CAP) * planes_pad : (k % CAP + 1) * planes_pad, :] = value
-
-    arrived[0 : CAP * planes_pad, :] = outbound[col]
-
-    def to_owner(step):
+
+    def to_owner(group, step):
         owner = lax.rem(col + step, ncol)
+        rows = CAP * level_groups(fields, levels)[group][2]
         return pltpu.make_async_remote_copy(
-            src_ref=outbound.at[owner],
-            dst_ref=arrived.at[pl.ds(step * CAP * planes_pad, CAP * planes_pad), :],
-            send_sem=out_sem.at[step],
-            recv_sem=in_sem.at[step],
+            src_ref=outbound[group].at[owner],
+            dst_ref=arrived[group].at[pl.ds(step * rows, rows), :],
+            send_sem=out_sem.at[group * ncol + step],
+            recv_sem=in_sem.at[group * ncol + step],
             device_id=(row, owner),
             device_id_type=MESH,
         )
 
-    for step in range(1, ncol):
-        to_owner(step).start()
-    for step in range(1, ncol):
-        to_owner(step).wait_recv()
+    for group, (start, stop, padded) in enumerate(level_groups(fields, levels)):
+        lax.fori_loop(start, stop, one_level, 0)
+        base = start * fields * tile_rows
+        sums = None
+        for t in range(tiles):
+            per_row = []
+            for g in range(coarse_rows):
+                value = None
+                for r in range(3 * g, 3 * g + 3):
+                    term = weighted[t, pl.ds(base + r, padded, stride=tile_rows), :]
+                    value = term if value is None else value + term
+                per_row.append(value)
+            fine = t * LANES + lax.broadcasted_iota(jnp.int32, (LANES, LANES), 0)
+            name = lax.broadcasted_iota(jnp.int32, (LANES, LANES), 1)
+            pick = (fine // 3 == name).astype(jnp.float32).astype(jnp.bfloat16)
+            term = split_dot(jnp.concatenate(per_row, 0), pick)
+            sums = term if sums is None else sums + term
+        size = coarse_rows * padded
+        coarse[0:size, :] = sums
+        tag_row = lax.broadcasted_iota(jnp.int32, (padded, LANES), 0) == (stop - start) * fields
+        blocks = []
+        for g in range(coarse_rows):
+            tag = (slot_ref[g] + 1).astype(jnp.float32)
+            blocks.append(jnp.where(tag_row, tag, coarse[g * padded : (g + 1) * padded, :]))
+        for k in range(ncol * CAP):
+            value = None
+            for g in range(coarse_rows):
+                term = jnp.where(spots[g] == k, 1.0, 0.0) * blocks[g]
+                value = term if value is None else value + term
+            outbound[group][k // CAP, (k % CAP) * padded : (k % CAP + 1) * padded, :] = value
+        for step in range(1, ncol):
+            to_owner(group, step).start()
+        arrived[group][0 : CAP * padded, :] = outbound[group][col]
+
+    groups = len(level_groups(fields, levels))
+    for group in range(groups):
+        for step in range(1, ncol):
+            to_owner(group, step).wait_recv()
 
     for way in range(8):
 
         @pl.when(exists(way))
         def _(way=way):
             remote(way).wait_send()
-
-    for step in range(1, ncol):
-        to_owner(step).wait_send()
-
-
-def finish(dims, nest, arrived, nest_hbm, parent_ref, store_sem):
-    planes, tiles, ncol = dims
-    planes_pad = round_up(planes, SUB)
+            if way in (NORTH, SOUTH):
+                for side in range(2):
+                    own_columns(way, side, False).wait_send()
+
+    for group in range(groups):
+        for step in range(1, ncol):
+            to_owner(group, step).wait_send()
+
+
+def finish(dims, nest, *refs):
+    fields, levels, tiles, ncol = dims
+    groups = level_groups(fields, levels)
+    arrived = refs[: len(groups)]
+    nest_hbm, parent_ref, store_sem = refs[len(groups) :]
     stores = []
     for t in range(tiles):
         copy = pltpu.make_async_copy(
@@ -379,7 +464,8 @@
         stores.append(copy)
 
     count = ncol * CAP
-    tags = arrived[pl.ds(planes, count, stride=planes_pad), :]
+    start, stop, padded = groups[0]
+    tags = arrived[0][pl.ds((stop - start) * fields, count, stride=padded), :]
     parent_row = lax.broadcasted_iota(jnp.int32, (count, LANES), 1).astype(jnp.float32) + 1.0
     picked = (tags == parent_row).astype(jnp.float32)
     stack = jnp.concatenate(
@@ -387,14 +473,18 @@
     )
     picker = stack.T[:PROWS].astype(jnp.bfloat16)
     filler = jnp.zeros((LANES - 2 * count, LANES), jnp.bfloat16)
-    for p in range(planes):
-        value = arrived[pl.ds(p, count, stride=planes_pad), :]
-        high = value.astype(jnp.bfloat16)
-        low = (value - high.astype(jnp.float32)).astype(jnp.bfloat16)
-        parent_ref[p] = jnp.dot(
-            picker, jnp.concatenate([high, low, filler], 0), preferred_element_type=jnp.float32
-        )
-
+    for ref, (start, stop, padded) in zip(arrived, groups):
+        for level in range(start, stop):
+            for f in range(fields):
+                at = (level - start) * fields + f
+                value = ref[pl.ds(at, count, stride=padded), :]
+                high = value.astype(jnp.bfloat16)
+                low = (value - high.astype(jnp.float32)).astype(jnp.bfloat16)
+                parent_ref[f * levels + level] = jnp.dot(
+                    picker,
+                    jnp.concatenate([high, low, filler], 0),
+                    preferred_element_type=jnp.float32,
+                )
     for copy in stores:
         copy.wait()
 
@@ -407,7 +497,7 @@
     planes_pad = round_up(planes, SUB)
     levels_pad = round_up(levels, SUB)
     total = 2 * planes_pad + 2 * levels_pad
-    own = (tiles, planes_pad * tile_rows, LANES)
+    own = (tiles, planes * tile_rows, LANES)
     level_own = (tiles, levels * tile_rows, LANES)
     f32 = jnp.float32
     vmem = pltpu.VMEM
@@ -415,14 +505,18 @@
     smem_spec = pl.BlockSpec(memory_space=pltpu.SMEM)
     any_spec = pl.BlockSpec(memory_space=pl.ANY)
     nest_shape = (tiles, planes * tile_rows, LANES)
-    arrived_shape = (ncol * CAP * planes_pad, LANES)
+    groups = level_groups(fields, levels)
+    reach = max(start * fields + padded for start, _, padded in groups)
+    most = max(padded for _, _, padded in groups)
     vmem_spec = pl.BlockSpec(memory_space=pltpu.VMEM)
-    nest, arrived = pl.pallas_call(
+    nest, *arrived = pl.pallas_call(
         functools.partial(kernel, (fields, levels, tile_rows, tiles)),
-        out_shape=(pltpu.VMEM(nest_shape, f32), pltpu.VMEM(arrived_shape, f32)),
+        out_shape=[pltpu.VMEM(nest_shape, f32)]
+        + [pltpu.VMEM((ncol * CAP * padded, LANES), f32) for _, _, padded in groups],
         in_specs=[smem_spec] * 3 + [any_spec] * 4,
-        out_specs=(vmem_spec, vmem_spec),
-        scratch_shapes=[
+        out_specs=[vmem_spec] * (1 + len(groups)),
+        scratch_shapes=[vmem((ncol, CAP * padded, LANES), f32) for _, _, padded in groups]
+        + [
             vmem(own, f32),
             vmem((tiles, planes * tile_rows, LANES), f32),
             vmem(level_own, f32),
@@ -430,18 +524,20 @@
             vmem((tiles, total * SUB, LANES), f32),
             vmem((tiles, tile_rows, LANES), f32),
             vmem((tiles, tile_rows, LANES), f32),
-            vmem((tile_rows // 3 * planes_pad, LANES), f32),
+            vmem((tile_rows // 3 * most, LANES), f32),
         ]
         + [vmem((ITERS * tiles, total, LANES), f32)] * 4
         + [vmem((3, tile_rows, LANES), f32)] * 4
         + [
             vmem((4, 3, SUB, LANES), f32),
-            vmem((ncol, CAP * planes_pad, LANES), f32),
+            vmem((4, 3, SUB, LANES), f32),
+            vmem((2, ITERS, tile_rows + SUB, LANES), f32),
+            vmem((tiles, reach * tile_rows, LANES), f32),
             dma((4 * tiles,)),
-            dma((8,)),
-            dma((8,)),
-            dma((ncol,)),
-            dma((ncol,)),
+            dma((12,)),
+            dma((12,)),
+            dma((len(groups) * ncol,)),
+            dma((len(groups) * ncol,)),
         ],
         compiler_params=pltpu.CompilerParams(
             collective_id=0, has_side_effects=True, vmem_limit_bytes=61 * 1024 * 1024
@@ -456,16 +552,16 @@
         advect_y.reshape(levels * tile_rows, tile_cols),
     )
     nest, parent = pl.pallas_call(
-        functools.partial(finish, (planes, tiles, ncol)),
+        functools.partial(finish, (fields, levels, tiles, ncol)),
         out_shape=(
             jax.ShapeDtypeStruct((planes * tile_rows, tile_cols), f32),
             jax.ShapeDtypeStruct((planes, PROWS, LANES), f32),
         ),
-        in_specs=[vmem_spec, vmem_spec],
+        in_specs=[vmem_spec] * (1 + len(groups)),
         out_specs=(any_spec, vmem_spec),
         scratch_shapes=[dma((tiles,))],
         compiler_params=pltpu.CompilerParams(vmem_limit_bytes=16 * 1024 * 1024),
-    )(nest, arrived)
+    )(nest, *arrived)
     return (
         nest.reshape(adjoint_field.shape),
         parent.reshape(fields, levels, PROWS, LANES),

time: 38 us -> 36.6 us (0.963)
  Pallas kernels: 37 us -> 35.8 us
    pallas_call x1, Pallas kernels: 34.5 us -> 33.4 us  [shards(): pl.pallas_call(functools.partial(kernel, (fields, levels, tile_rows, tile...]
where the time goes in v3:
time: 36.6 us; the launch traced here: 36.5 us
  Pallas kernels  35.8 us (98%)
  between operations  0.64 us (2%)
    pallas_call x1, Pallas kernels, shards(): pl.pallas_call(functools.partial(kernel, (fields, levels, tile_rows, tile...  33.4 us
    pallas_call x1, Pallas kernels, shards(): pl.pallas_call(functools.partial(finish, (fields, levels, tiles, ncol)),...  2.43 us

profile of v3, /device:TPU:1, one launch (start us, length us, event | category | flops | bytes accessed | tf_op | source)
XLA Modules:
  0.0 36.5 jit_solution(8634175520058882300)
XLA Ops:
  0.6 33.4 %shard_map.86 = (f32[3,1440,128]{2,1,0:T(8,128)S(1)}, f32[256,128]{1,0:T(8,128)S(1)}, f32[256,128]{1,0:T(8,128)S(1)}, f32[128,128]{1,0:T(8,128)S(1)}) custom-call(s32[4]{0:T(128)} %zone_ref.1, s32[16]{0:T(128)} %bitcast.12, s32[16]{0:T(128)} %bitcast.13, f32[1440,384]{1,0:T(8,128)} %bitcast.8, f32[1440,384]{1,0:T(8,128)} %bitcast.9, f32[288,384]{1,0:T(8,128)} %bitcast.10, ...), custom_call_target="tpu_custom_call" | custom-call | tf_op jit(solution)/shard_map/pallas_call | solution.py:512
  34.0 2.4 %shard_map.87 = (f32[1440,384]{1,0:T(8,128)}, f32[30,80,128]{2,1,0:T(8,128)}) custom-call(f32[3,1440,128]{2,1,0:T(8,128)S(1)} %get-tuple-element.8.nest, f32[256,128]{1,0:T(8,128)S(1)} %get-tuple-element.9.refs_0_, f32[256,128]{1,0:T(8,128)S(1)} %get-tuple-element.10.refs_1_, f32[128,128]{1,0:T(8,128)S(1)} %get-tuple-element.11.refs_2_), custom_call_target="tpu_custom_call" | custom-call | tf_op jit(solution)/shard_map/pallas_call | solution.py:554

commit v4 on v3

--- a/solution.py
+++ b/solution.py
@@ -189,6 +189,58 @@
         slab_w[kind] = first
         slab_e[kind] = last
 
+    top, bottom = slice(0, SUB), slice(tile_rows - SUB, tile_rows)
+    sources = {
+        NORTH: rows_n,
+        SOUTH: rows_s,
+        EAST: slab_e,
+        WEST: slab_w,
+        NE: slab_e.at[:, top, :],
+        NW: slab_w.at[:, top, :],
+        SE: slab_e.at[:, bottom, :],
+        SW: slab_w.at[:, bottom, :],
+    }
+
+    def remote(way):
+        back = OPPOSITE[way]
+        return pltpu.make_async_remote_copy(
+            src_ref=sources[way],
+            dst_ref=received[back],
+            send_sem=send_sem.at[way],
+            recv_sem=recv_sem.at[back],
+            device_id=device(way),
+            device_id_type=MESH,
+        )
+
+    def own_columns(way, side, arriving):
+        back = OPPOSITE[way]
+        sent = back if arriving else way
+        place = 2 * side + (way if arriving else back)
+        slab = (slab_e, slab_w)[side]
+        return pltpu.make_async_remote_copy(
+            src_ref=slab.at[:, top if sent == NORTH else bottom, :],
+            dst_ref=got_own.at[place],
+            send_sem=send_sem.at[8 + 2 * side + sent],
+            recv_sem=recv_sem.at[8 + place],
+            device_id=device(way),
+            device_id_type=MESH,
+        )
+
+    greeted = jnp.int32(ncol - 1)
+    for way in (NORTH, SOUTH, NE, NW, SE, SW):
+        greeted = greeted + exists(way).astype(jnp.int32)
+    pl.semaphore_wait(barrier, greeted)
+
+    for way in range(8):
+
+        @pl.when(exists(way))
+        def _(way=way):
+            if way in (NORTH, SOUTH):
+                for side in range(2):
+                    own_columns(way, side, False).start()
+            else:
+                remote(way).start()
+
     for r in range(ITERS):
         for t in range(tiles):
             for source, count, base in (
@@ -204,55 +256,10 @@
                     t, pl.ds(tile_rows - ITERS + r, count, stride=tile_rows), :
                 ]
 
-    top, bottom = slice(0, SUB), slice(tile_rows - SUB, tile_rows)
-    sources = {
-        NORTH: rows_n,
-        SOUTH: rows_s,
-        EAST: slab_e,
-        WEST: slab_w,
-        NE: slab_e.at[:, top, :],
-        NW: slab_w.at[:, top, :],
-        SE: slab_e.at[:, bottom, :],
-        SW: slab_w.at[:, bottom, :],
-    }
-
-    def remote(way):
-        back = OPPOSITE[way]
-        return pltpu.make_async_remote_copy(
-            src_ref=sources[way],
-            dst_ref=received[back],
-            send_sem=send_sem.at[way],
-            recv_sem=recv_sem.at[back],
-            device_id=device(way),
-            device_id_type=MESH,
-        )
-
-    def own_columns(way, side, arriving):
-        back = OPPOSITE[way]
-        sent = back if arriving else way
-        place = 2 * side + (way if arriving else back)
-        slab = (slab_e, slab_w)[side]
-        return pltpu.make_async_remote_copy(
-            src_ref=slab.at[:, top if sent == NORTH else bottom, :],
-            dst_ref=got_own.at[place],
-            send_sem=send_sem.at[8 + 2 * side + sent],
-            recv_sem=recv_sem.at[8 + place],
-            device_id=device(way),
-            device_id_type=MESH,
-        )
-
-    greeted = jnp.int32(ncol - 1)
-    for way in (NORTH, SOUTH, NE, NW, SE, SW):
-        greeted = greeted + exists(way).astype(jnp.int32)
-    pl.semaphore_wait(barrier, greeted)
-
-    for way in range(8):
+    for way in (NORTH, SOUTH):
 
         @pl.when(exists(way))
         def _(way=way):
-            if way in (NORTH, SOUTH):
-                for side in range(2):
-                    own_columns(way, side, False).start()
             remote(way).start()
 
     for way in range(8):

time: 36.6 us -> 36.5 us (level)
  no operation moved by 1% of the time
where the time goes in v4:
time: 36.5 us; the launch traced here: 36.4 us
  Pallas kernels  35.7 us (98%)
  between operations  0.64 us (2%)
    pallas_call x1, Pallas kernels, shards(): pl.pallas_call(functools.partial(kernel, (fields, levels, tile_rows, tile...  33.3 us
    pallas_call x1, Pallas kernels, shards(): pl.pallas_call(functools.partial(finish, (fields, levels, tiles, ncol)),...  2.43 us

profile of v4, /device:TPU:1, one launch (start us, length us, event | category | flops | bytes accessed | tf_op | source)
XLA Modules:
  0.0 36.4 jit_solution(3274291489707648220)
XLA Ops:
  0.6 33.3 %shard_map.86 = (f32[3,1440,128]{2,1,0:T(8,128)S(1)}, f32[256,128]{1,0:T(8,128)S(1)}, f32[256,128]{1,0:T(8,128)S(1)}, f32[128,128]{1,0:T(8,128)S(1)}) custom-call(s32[4]{0:T(128)} %zone_ref.1, s32[16]{0:T(128)} %bitcast.12, s32[16]{0:T(128)} %bitcast.13, f32[1440,384]{1,0:T(8,128)} %bitcast.8, f32[1440,384]{1,0:T(8,128)} %bitcast.9, f32[288,384]{1,0:T(8,128)} %bitcast.10, ...), custom_call_target="tpu_custom_call" | custom-call | tf_op jit(solution)/shard_map/pallas_call | solution.py:519
  33.9 2.4 %shard_map.87 = (f32[1440,384]{1,0:T(8,128)}, f32[30,80,128]{2,1,0:T(8,128)}) custom-call(f32[3,1440,128]{2,1,0:T(8,128)S(1)} %get-tuple-element.8.nest, f32[256,128]{1,0:T(8,128)S(1)} %get-tuple-element.9.refs_0_, f32[256,128]{1,0:T(8,128)S(1)} %get-tuple-element.10.refs_1_, f32[128,128]{1,0:T(8,128)S(1)} %get-tuple-element.11.refs_2_), custom_call_target="tpu_custom_call" | custom-call | tf_op jit(solution)/shard_map/pallas_call | solution.py:561
